TPU v7x, 32 devices: a whole 2x2x4 slice. The times are simulated.
32 devices in a mesh: vec: 8 (over z, core), rep: 4 (over y, x).
Axes of the slice: x: 2, y: 2, z: 4, core: 2. Of those that a mesh axis runs over, the one named last changes fastest.
Arguments:
- vectors: bfloat16 [1024, 1024], P('vec'), may hold values from 0 to 2
- pivot_index: int32 [4, 8], P('rep'), may hold values from 0 to 1023
Outputs:
- similarity: bfloat16 [7, 32, 1024, 128], P(None, 'rep', 'vec')
All inputs are finite; a program needn't handle non-finite values.
Results may differ from a plain program's by a relative error of at most 0.011.
Values may be sent and summed in bfloat16 or wider, within the bound.
A program may use at most 64 MiB of HBM per device.

v0:
```python
import math
import jax
import jax.numpy as jnp
from jax import lax
from jax.sharding import PartitionSpec as P

HALF = 3


def from_behind(block, axis, distance):
    devices = range(lax.axis_size(axis))
    route = [((i - distance) % len(devices), i) for i in devices]
    return lax.ppermute(block, axis, route)


def contract(left, right):
    return lax.dot_general(
        left, right, (((1,), (1,)), ((), ())), preferred_element_type=jnp.float32
    )


def on_device(vectors, pivot_index):
    block_rows, fields = vectors.shape
    position = lax.axis_index("vec")
    wanted = pivot_index.reshape(-1) - position * block_rows
    columns = jnp.arange(block_rows, dtype=jnp.int32)
    onehot = (wanted[:, None] == columns[None, :]).astype(jnp.bfloat16)
    local_rows = jnp.dot(onehot, vectors, preferred_element_type=jnp.float32)
    pivots = lax.psum(local_rows, "vec")
    count = pivots.shape[0]
    centre = jnp.sum(pivots, axis=1) / fields
    scaled = (vectors.astype(jnp.float32)[None, :, :] * pivots[:, None, :]).astype(jnp.bfloat16)
    scaled = scaled.reshape(count * block_rows, fields)
    replicas = lax.axis_size("rep")
    share = block_rows // replicas
    own_rows = lax.dynamic_slice_in_dim(vectors, lax.axis_index("rep") * share, share, 0)
    window = 2 * HALF + 1
    triples = [None] * window
    grams = [None] * window
    triples[HALF] = contract(scaled, vectors)
    grams[HALF] = contract(own_rows, vectors)
    lower = vectors
    upper = vectors
    for reach in range(1, HALF + 1):
        lower = from_behind(lower, "vec", 1)
        upper = from_behind(upper, "vec", -1)
        triples[HALF - reach] = contract(scaled, lower)
        grams[HALF - reach] = contract(own_rows, lower)
        triples[HALF + reach] = contract(scaled, upper)
        grams[HALF + reach] = contract(own_rows, upper)
    triple_all = jnp.stack(triples).reshape(window, count, block_rows, block_rows)
    gram_all = jnp.stack(grams)
    gram_all = lax.all_gather(gram_all, "rep", axis=1, tiled=True)
    similarity = (triple_all - centre[None, :, None, None] * gram_all[:, None, :, :]) / math.sqrt(
        fields
    )
    return similarity.astype(jnp.bfloat16)


def solution(mesh):
    in_specs = (P("vec", None), P("rep", None))
    out_specs = P(None, "rep", "vec", None)
    return jax.shard_map(
        on_device, mesh=mesh, in_specs=in_specs, out_specs=out_specs, check_vma=False
    )
```

profile of v0, /device:TPU:0, one launch (start us, length us, event | category | flops | bytes accessed | tf_op | source)
XLA Modules:
  0.0 71.4 jit_solution(5123657337619987184)
XLA Ops:
  0.0 0.5 collective-permute-start
  0.5 4.0 %collective-permute-start.3 = (bf16[128,1024]{1,0:T(8,128)(2,1)}, bf16[128,1024]{1,0:T(8,128)(2,1)S(1)}, u32[]{:S(2)}, u32[]{:S(2)}) collective-permute-start(bf16[128,1024]{1,0:T(8,128)(2,1)} %param.2), channel_id=1, source_target_pairs={{4,0},{8,4},{12,8},{16,12},{20,16},{24,20},{28,24},{0,28},{5,1},{9... | collective-permute-start | bytes 786440 | tf_op jit(solution)/shard_map/ppermute | solution.py:13
  4.5 4.5 %collective-permute-done = bf16[128,1024]{1,0:T(8,128)(2,1)S(1)} collective-permute-done((bf16[128,1024]{1,0:T(8,128)(2,1)}, bf16[128,1024]{1,0:T(8,128)(2,1)S(1)}, u32[]{:S(2)}, u32[]{:S(2)}) %collective-permute-start) | collective-permute-done | bytes 262176 | tf_op jit(solution)/shard_map/ppermute | solution.py:13
  9.0 0.7 subtract_bitcast_fusion
  9.7 3.5 %collective-permute-start.4 = (bf16[128,1024]{1,0:T(8,128)(2,1)S(1)}, bf16[128,1024]{1,0:T(8,128)(2,1)S(1)}, u32[]{:S(2)}, u32[]{:S(2)}) collective-permute-start(bf16[128,1024]{1,0:T(8,128)(2,1)S(1)} %collective-permute-done.3), channel_id=1, source_target_pairs={{4,0},{8,4},{12,8},{16,12},{20,16},{24,20},{28,24},{0,28},{5,1},{9... | collective-permute-start | bytes 786440 | tf_op jit(solution)/shard_map/ppermute | solution.py:13
  13.2 3.5 %collective-permute-done.1 = bf16[128,1024]{1,0:T(8,128)(2,1)S(1)} collective-permute-done((bf16[128,1024]{1,0:T(8,128)(2,1)S(1)}, bf16[128,1024]{1,0:T(8,128)(2,1)S(1)}, u32[]{:S(2)}, u32[]{:S(2)}) %collective-permute-start.1) | collective-permute-done | bytes 262176 | tf_op jit(solution)/shard_map/ppermute | solution.py:13
  16.7 1.1 %fusion.56 = f32[8,1024]{1,0:T(8,128)S(1)} fusion(bf16[128,1024]{1,0:T(8,128)(2,1)} %param.2, s32[8]{0:T(128)S(1)} %subtract_bitcast_fusion), kind=kOutput, calls=%fused_computation.66 | convolution fusion | flops 2098176 | bytes 294944 | tf_op jit(solution)/shard_map/dot_general | solution.py:28
  17.8 1.0 %convert_element_type.21 = f32[128,1024]{1,0:T(8,128)S(1)} convert(bf16[128,1024]{1,0:T(8,128)(2,1)} %param.2) | non-fusion elementwise | flops 131072 | bytes 786432 | tf_op jit(solution)/shard_map/convert_element_type | solution.py:32
  18.8 29.4 %psum.7 = f32[8,1024]{1,0:T(8,128)S(1)} all-reduce(f32[8,1024]{1,0:T(8,128)S(1)} %fusion.56), channel_id=1, replica_groups=mesh['vec'=8,'rep'=4] {'vec'}, use_global_device_ids=true, to_apply=%region_0.0 | all-reduce | flops 8192 | bytes 65536 | tf_op jit(solution)/shard_map/psum | solution.py:29
  48.5 1.0 %fusion.41 = f32[7,32,128]{2,1,0:T(8,128)S(1)} fusion(bf16[128,1024]{1,0:T(8,128)(2,1)S(1)} %collective-permute-done.2, bf16[128,1024]{1,0:T(8,128)(2,1)} %param.2, s32[]{:T(128)S(6)} %select_n.3), kind=kOutput, calls=%fused_computation.50 | convolution fusion | flops 8388607 | bytes 344068 | tf_op jit(solution)/shard_map/dot_general | solution.py:17
  49.5 1.0 %fusion.40 = f32[7,32,128]{2,1,0:T(8,128)S(1)} fusion(f32[7,32,128]{2,1,0:T(8,128)S(1)} %fusion.41, bf16[128,1024]{1,0:T(8,128)(2,1)S(1)} %collective-permute-done.1, bf16[128,1024]{1,0:T(8,128)(2,1)} %param.2, s32[]{:T(128)S(6)} %select_n.3), kind=kOutput, calls=%fused_computation.48 | convolution fusion | flops 8388608 | bytes 344068 | tf_op jit(solution)/shard_map/dot_general | solution.py:17
  50.5 1.0 %fusion.39 = f32[7,32,128]{2,1,0:T(8,128)S(1)} fusion(f32[7,32,128]{2,1,0:T(8,128)S(1)} %fusion.40, bf16[128,1024]{1,0:T(8,128)(2,1)S(1)} %collective-permute-done, bf16[128,1024]{1,0:T(8,128)(2,1)} %param.2, s32[]{:T(128)S(6)} %select_n.3), kind=kOutput, calls=%fused_computation.46 | convolution fusion | flops 8388608 | bytes 344068 | tf_op jit(solution)/shard_map/dot_general | solution.py:17
  51.6 1.2 %fusion.38 = f32[7,32,128]{2,1,0:T(8,128)S(1)} fusion(f32[7,32,128]{2,1,0:T(8,128)S(1)} %fusion.39, bf16[128,1024]{1,0:T(8,128)(2,1)} %param.2, s32[]{:T(128)S(6)} %select_n.3), kind=kOutput, calls=%fused_computation.44 | convolution fusion | flops 8388608 | bytes 344068 | tf_op jit(solution)/shard_map/dot_general | solution.py:17
  52.8 0.7 %fusion.22 = f32[7,8,128,128]{3,2,1,0:T(8,128)S(1)} fusion(f32[8,1024]{1,0:T(8,128)S(1)} %psum.7, f32[128,1024]{1,0:T(8,128)S(1)} %convert_element_type.21, bf16[128,1024]{1,0:T(8,128)(2,1)S(1)} %collective-permute-done.2), kind=kOutput, calls=%fused_computation.24 | convolution fusion | flops 270532608 | bytes 1343488 | tf_op jit(solution)/shard_map/dot_general | solution.py:17
  53.6 0.7 fusion.24
  54.3 0.7 fusion.26
  55.2 0.2 fusion.36
  55.4 0.7 %fusion.28 = f32[7,8,128,128]{3,2,1,0:T(8,128)S(1)} fusion(f32[7,8,128,128]{3,2,1,0:T(8,128)S(1)} %fusion.26, f32[8,1024]{1,0:T(8,128)S(1)} %psum.7, f32[128,1024]{1,0:T(8,128)S(1)} %convert_element_type.21, bf16[128,1024]{1,0:T(8,128)(2,1)S(1)} %copy-done), kind=kOutput, calls=%fused_computation.30 | convolution fusion | flops 270532608 | bytes 1343488 | tf_op jit(solution)/shard_map/dot_general | solution.py:17
  56.1 0.2 fusion.35
  56.3 11.0 %all_gather.3 = f32[7,128,128]{2,1,0:T(8,128)S(1)} all-gather(f32[7,32,128]{2,1,0:T(8,128)S(1)} %fusion.35), channel_id=1, replica_groups=mesh['vec'=8,'rep'=4] {'rep'}, dimensions={1}, use_global_device_ids=true | all-gather | bytes 573440 | tf_op jit(solution)/shard_map/all_gather | solution.py:53
  67.3 0.7 fusion.30
  68.0 0.7 fusion.32
  68.8 0.7 fusion.34
  69.5 1.9 %multiply_convert_fusion.8 = bf16[7,8,128,128]{3,2,1,0:T(8,128)(2,1)} fusion(f32[7,8,128,128]{3,2,1,0:T(8,128)S(1)} %fusion.34, f32[7,128,128]{2,1,0:T(8,128)S(1)} %all_gather.3, f32[8]{0:T(128)S(1)} %broadcast_multiply_fusion), kind=kLoop, calls=%fused_computation.8 | loop fusion | flops 3670016 | bytes 5963808 | tf_op jit(solution)/shard_map/convert_element_type | solution.py:57
  (12 shorter events, 0.4 us)
Async XLA Ops:
  0.0 9.0 %collective-permute-start = (bf16[128,1024]{1,0:T(8,128)(2,1)}, bf16[128,1024]{1,0:T(8,128)(2,1)S(1)}, u32[]{:S(2)}, u32[]{:S(2)}) collective-permute-start(bf16[128,1024]{1,0:T(8,128)(2,1)} %param.2), channel_id=1, source_target_pairs={{28,0},{0,4},{4,8},{8,12},{12,16},{16,20},{20,24},{24,28},{29,1},{... | collective-permute-start | bytes 786440 | tf_op jit(solution)/shard_map/ppermute | solution.py:13
  0.5 9.2 %collective-permute-start.3 = (bf16[128,1024]{1,0:T(8,128)(2,1)}, bf16[128,1024]{1,0:T(8,128)(2,1)S(1)}, u32[]{:S(2)}, u32[]{:S(2)}) collective-permute-start(bf16[128,1024]{1,0:T(8,128)(2,1)} %param.2), channel_id=1, source_target_pairs={{4,0},{8,4},{12,8},{16,12},{20,16},{24,20},{28,24},{0,28},{5,1},{9... | collective-permute-start | bytes 786440 | tf_op jit(solution)/shard_map/ppermute | solution.py:13
  9.0 7.7 %collective-permute-start.1 = (bf16[128,1024]{1,0:T(8,128)(2,1)S(1)}, bf16[128,1024]{1,0:T(8,128)(2,1)S(1)}, u32[]{:S(2)}, u32[]{:S(2)}) collective-permute-start(bf16[128,1024]{1,0:T(8,128)(2,1)S(1)} %collective-permute-done), channel_id=1, source_target_pairs={{28,0},{0,4},{4,8},{8,12},{12,16},{16,20},{20,24},{24,28},{29,1},{... | collective-permute-start | bytes 786440 | tf_op jit(solution)/shard_map/ppermute | solution.py:13
  9.7 38.7 %collective-permute-start.4 = (bf16[128,1024]{1,0:T(8,128)(2,1)S(1)}, bf16[128,1024]{1,0:T(8,128)(2,1)S(1)}, u32[]{:S(2)}, u32[]{:S(2)}) collective-permute-start(bf16[128,1024]{1,0:T(8,128)(2,1)S(1)} %collective-permute-done.3), channel_id=1, source_target_pairs={{4,0},{8,4},{12,8},{16,12},{20,16},{24,20},{28,24},{0,28},{5,1},{9... | collective-permute-start | bytes 786440 | tf_op jit(solution)/shard_map/ppermute | solution.py:13
  16.7 31.8 %collective-permute-start.2 = (bf16[128,1024]{1,0:T(8,128)(2,1)S(1)}, bf16[128,1024]{1,0:T(8,128)(2,1)S(1)}, u32[]{:S(2)}, u32[]{:S(2)}) collective-permute-start(bf16[128,1024]{1,0:T(8,128)(2,1)S(1)} %collective-permute-done.1), channel_id=1, source_target_pairs={{28,0},{0,4},{4,8},{8,12},{12,16},{16,20},{20,24},{24,28},{29,1},{... | collective-permute-start | bytes 786440 | tf_op jit(solution)/shard_map/ppermute | solution.py:13
  48.4 7.7 %collective-permute-start.5 = (bf16[128,1024]{1,0:T(8,128)(2,1)S(1)}, bf16[128,1024]{1,0:T(8,128)(2,1)S(1)}, u32[]{:S(2)}, u32[]{:S(2)}) collective-permute-start(bf16[128,1024]{1,0:T(8,128)(2,1)S(1)} %collective-permute-done.4), channel_id=1, source_target_pairs={{4,0},{8,4},{12,8},{16,12},{20,16},{24,20},{28,24},{0,28},{5,1},{9... | collective-permute-start | bytes 786440 | tf_op jit(solution)/shard_map/ppermute | solution.py:13
  52.8 2.2 %copy-start = (bf16[128,1024]{1,0:T(8,128)(2,1)S(1)}, bf16[128,1024]{1,0:T(8,128)(2,1)}, u32[]{:S(2)}) copy-start(bf16[128,1024]{1,0:T(8,128)(2,1)} %param.2) | copy-start | bytes 786436
where the time goes:
time: 71.7 us; the launch traced here: 71.4 us
  blocking collectives  40.5 us (56%)
  matrix products  11 us (15%)
  starting transfers between devices  8.13 us (11%)
  waiting for transfers between devices  7.96 us (11%)
  other arithmetic  3.69 us (5%)
    psum x1, blocking collectives, on_device(): pivots = lax.psum(local_rows, 'vec')  29.4 us
    all_gather x1, blocking collectives, on_device(): gram_all = lax.all_gather(gram_all, 'rep', axis=1, tiled=True)  11 us
    dot_general x14, matrix products, contract(): lax.dot_general(left, right, (((1,), (1,)), ((), ())), preferred_element_...  9.87 us
    ppermute x6, starting transfers between devices, from_behind(): return lax.ppermute(block, axis, route)  8.13 us
    ppermute x6, waiting for transfers between devices, from_behind(): return lax.ppermute(block, axis, route)  7.96 us
    convert_element_type x1, other arithmetic, on_device(): return similarity.astype(jnp.bfloat16)  1.9 us
  transfers between devices with their start and end apart: 6, of which 2 were waited for; matrix products, arithmetic and copies ran while one was open for 15% of the time, Pallas kernels for 0%

commit v1 on v0

--- a/solution.py
+++ b/solution.py
@@ -5,6 +5,15 @@
 from jax.sharding import PartitionSpec as P
 
 HALF = 3
+
+
+def sum_by_hops(x, axis):
+    devices = lax.axis_size(axis)
+    total, far = (x, 1)
+    while far < devices:
+        total = total + lax.ppermute(total, axis, [(i, i ^ far) for i in range(devices)])
+        far = 2 * far
+    return total
 
 
 def from_behind(block, axis, distance):
@@ -26,7 +35,7 @@
     columns = jnp.arange(block_rows, dtype=jnp.int32)
     onehot = (wanted[:, None] == columns[None, :]).astype(jnp.bfloat16)
     local_rows = jnp.dot(onehot, vectors, preferred_element_type=jnp.float32)
-    pivots = lax.psum(local_rows, "vec")
+    pivots = sum_by_hops(local_rows, "vec")
     count = pivots.shape[0]
     centre = jnp.sum(pivots, axis=1) / fields
     scaled = (vectors.astype(jnp.float32)[None, :, :] * pivots[:, None, :]).astype(jnp.bfloat16)

time: 71.7 us -> 54 us (0.75)
  blocking collectives: 40.5 us -> 9.8 us
  starting transfers between devices: 8.13 us -> 16.3 us
  waiting for transfers between devices: 7.96 us -> 12.6 us
    psum x1 -> x0, blocking collectives: 29.4 us -> none  [on_device(): pivots = lax.psum(local_rows, 'vec')]
    ppermute x0 -> x3, starting transfers between devices: none -> 7.6 us  [sum_by_hops(): lax.ppermute(total, axis, [(i, i ^ far) for i in range(devices)])]
    ppermute x0 -> x3, waiting for transfers between devices: none -> 3.07 us  [sum_by_hops(): lax.ppermute(total, axis, [(i, i ^ far) for i in range(devices)])]
    ppermute x6, waiting for transfers between devices: 7.96 us -> 9.57 us  [from_behind(): return lax.ppermute(block, axis, route)]
    all_gather x1, blocking collectives: 11 us -> 9.8 us  [on_device(): gram_all = lax.all_gather(gram_all, 'rep', axis=1, tiled=True)]
  transfers between devices with their start and end apart: 6 -> 9, of which waited for: 2 -> 5; matrix products, arithmetic and copies ran while one was open for 15% -> 20% of each run, Pallas kernels for 0% -> 0%
where the time goes in v1:
time: 54 us; the launch traced here: 53.6 us
  starting transfers between devices  16.3 us (30%)
  waiting for transfers between devices  12.6 us (23%)
  matrix products  11 us (20%)
  blocking collectives  9.8 us (18%)
  other arithmetic  3.69 us (7%)
    dot_general x14, matrix products, contract(): lax.dot_general(left, right, (((1,), (1,)), ((), ())), preferred_element_...  9.87 us
    all_gather x1, blocking collectives, on_device(): gram_all = lax.all_gather(gram_all, 'rep', axis=1, tiled=True)  9.8 us
    ppermute x6, waiting for transfers between devices, from_behind(): return lax.ppermute(block, axis, route)  9.57 us
    ppermute x6, starting transfers between devices, from_behind(): return lax.ppermute(block, axis, route)  8.75 us
    ppermute x3, starting transfers between devices, sum_by_hops(): lax.ppermute(total, axis, [(i, i ^ far) for i in range(devices)])  7.6 us
    ppermute x3, waiting for transfers between devices, sum_by_hops(): lax.ppermute(total, axis, [(i, i ^ far) for i in range(devices)])  3.07 us
    convert_element_type x1, other arithmetic, on_device(): return similarity.astype(jnp.bfloat16)  1.9 us
    dot_general x1, matrix products, on_device(): local_rows = jnp.dot(onehot, vectors, preferred_element_type=jnp.float32)  1.14 us
  transfers between devices with their start and end apart: 9, of which 5 were waited for; matrix products, arithmetic and copies ran while one was open for 20% of the time, Pallas kernels for 0%

profile of v1, /device:TPU:0, one launch (start us, length us, event | category | flops | bytes accessed | tf_op | source)
XLA Modules:
  0.0 53.6 jit_solution(14228635972462127360)
XLA Ops:
  0.5 4.0 %collective-permute-start.6 = (bf16[128,1024]{1,0:T(8,128)(2,1)}, bf16[128,1024]{1,0:T(8,128)(2,1)S(1)}, u32[]{:S(2)}, u32[]{:S(2)}) collective-permute-start(bf16[128,1024]{1,0:T(8,128)(2,1)} %param.2), channel_id=1, source_target_pairs={{4,0},{8,4},{12,8},{16,12},{20,16},{24,20},{28,24},{0,28},{5,1},{9... | collective-permute-start | bytes 786440 | tf_op jit(solution)/shard_map/ppermute | solution.py:22
  5.2 3.8 %collective-permute-done.3 = bf16[128,1024]{1,0:T(8,128)(2,1)S(1)} collective-permute-done((bf16[128,1024]{1,0:T(8,128)(2,1)}, bf16[128,1024]{1,0:T(8,128)(2,1)S(1)}, u32[]{:S(2)}, u32[]{:S(2)}) %collective-permute-start.3) | collective-permute-done | bytes 262176 | tf_op jit(solution)/shard_map/ppermute | solution.py:22
  9.0 1.1 %fusion.56 = f32[8,1024]{1,0:T(8,128)S(1)} fusion(bf16[128,1024]{1,0:T(8,128)(2,1)} %param.2, s32[8]{0:T(128)S(1)} %subtract_bitcast_fusion), kind=kOutput, calls=%fused_computation.66 | convolution fusion | flops 2098176 | bytes 294944 | tf_op jit(solution)/shard_map/dot_general | solution.py:37
  10.1 1.0 %collective-permute-start = (f32[8,1024]{1,0:T(8,128)S(1)}, f32[8,1024]{1,0:T(8,128)S(1)}, u32[]{:S(2)}, u32[]{:S(2)}) collective-permute-start(f32[8,1024]{1,0:T(8,128)S(1)} %fusion.56), channel_id=1, source_target_pairs={{0,4},{4,0},{8,12},{12,8},{16,20},{20,16},{24,28},{28,24},{1,5},{5... | collective-permute-start | bytes 98312 | tf_op jit(solution)/shard_map/ppermute | solution.py:14
  11.1 0.9 %collective-permute-done = f32[8,1024]{1,0:T(8,128)S(1)} collective-permute-done((f32[8,1024]{1,0:T(8,128)S(1)}, f32[8,1024]{1,0:T(8,128)S(1)}, u32[]{:S(2)}, u32[]{:S(2)}) %collective-permute-start) | collective-permute-done | bytes 32800 | tf_op jit(solution)/shard_map/ppermute | solution.py:14
  12.0 3.6 %collective-permute-start.1 = (f32[8,1024]{1,0:T(8,128)S(1)}, f32[8,1024]{1,0:T(8,128)S(1)}, u32[]{:S(2)}, u32[]{:S(2)}) collective-permute-start(f32[8,1024]{1,0:T(8,128)S(1)} %add.12), channel_id=1, source_target_pairs={{0,8},{4,12},{8,0},{12,4},{16,24},{20,28},{24,16},{28,20},{1,9},{5... | collective-permute-start | bytes 98312 | tf_op jit(solution)/shard_map/ppermute | solution.py:14
  15.6 1.9 %collective-permute-done.1 = f32[8,1024]{1,0:T(8,128)S(1)} collective-permute-done((f32[8,1024]{1,0:T(8,128)S(1)}, f32[8,1024]{1,0:T(8,128)S(1)}, u32[]{:S(2)}, u32[]{:S(2)}) %collective-permute-start.1) | collective-permute-done | bytes 32800 | tf_op jit(solution)/shard_map/ppermute | solution.py:14
  17.5 3.0 %collective-permute-start.2 = (f32[8,1024]{1,0:T(8,128)S(1)}, f32[8,1024]{1,0:T(8,128)S(1)}, u32[]{:S(2)}, u32[]{:S(2)}) collective-permute-start(f32[8,1024]{1,0:T(8,128)S(1)} %add.13), channel_id=1, source_target_pairs={{0,16},{4,20},{8,24},{12,28},{16,0},{20,4},{24,8},{28,12},{1,17},{... | collective-permute-start | bytes 98312 | tf_op jit(solution)/shard_map/ppermute | solution.py:14
  20.5 1.0 %convert_element_type.21 = f32[128,1024]{1,0:T(8,128)S(1)} convert(bf16[128,1024]{1,0:T(8,128)(2,1)} %param.2) | non-fusion elementwise | flops 131072 | bytes 786432 | tf_op jit(solution)/shard_map/convert_element_type | solution.py:41
  22.5 5.7 %collective-permute-done.7 = bf16[128,1024]{1,0:T(8,128)(2,1)S(1)} collective-permute-done((bf16[128,1024]{1,0:T(8,128)(2,1)S(1)}, bf16[128,1024]{1,0:T(8,128)(2,1)S(1)}, u32[]{:S(2)}, u32[]{:S(2)}) %collective-permute-start.7) | collective-permute-done | bytes 262176 | tf_op jit(solution)/shard_map/ppermute | solution.py:22
  28.3 3.7 %collective-permute-start.8 = (bf16[128,1024]{1,0:T(8,128)(2,1)S(1)}, bf16[128,1024]{1,0:T(8,128)(2,1)S(1)}, u32[]{:S(2)}, u32[]{:S(2)}) collective-permute-start(bf16[128,1024]{1,0:T(8,128)(2,1)S(1)} %collective-permute-done.7), channel_id=1, source_target_pairs={{4,0},{8,4},{12,8},{16,12},{20,16},{24,20},{28,24},{0,28},{5,1},{9... | collective-permute-start | bytes 786440 | tf_op jit(solution)/shard_map/ppermute | solution.py:22
  32.0 1.0 %fusion.41 = f32[7,32,128]{2,1,0:T(8,128)S(1)} fusion(bf16[128,1024]{1,0:T(8,128)(2,1)S(1)} %collective-permute-done.5, bf16[128,1024]{1,0:T(8,128)(2,1)} %param.2, s32[]{:T(128)S(6)} %select_n.3), kind=kOutput, calls=%fused_computation.50 | convolution fusion | flops 8388607 | bytes 344068 | tf_op jit(solution)/shard_map/dot_general | solution.py:26
  33.0 1.0 %fusion.40 = f32[7,32,128]{2,1,0:T(8,128)S(1)} fusion(f32[7,32,128]{2,1,0:T(8,128)S(1)} %fusion.41, bf16[128,1024]{1,0:T(8,128)(2,1)S(1)} %collective-permute-done.4, bf16[128,1024]{1,0:T(8,128)(2,1)} %param.2, s32[]{:T(128)S(6)} %select_n.3), kind=kOutput, calls=%fused_computation.48 | convolution fusion | flops 8388608 | bytes 344068 | tf_op jit(solution)/shard_map/dot_general | solution.py:26
  34.0 1.0 %fusion.39 = f32[7,32,128]{2,1,0:T(8,128)S(1)} fusion(f32[7,32,128]{2,1,0:T(8,128)S(1)} %fusion.40, bf16[128,1024]{1,0:T(8,128)(2,1)S(1)} %collective-permute-done.3, bf16[128,1024]{1,0:T(8,128)(2,1)} %param.2, s32[]{:T(128)S(6)} %select_n.3), kind=kOutput, calls=%fused_computation.46 | convolution fusion | flops 8388608 | bytes 344068 | tf_op jit(solution)/shard_map/dot_general | solution.py:26
  35.1 1.2 %fusion.38 = f32[7,32,128]{2,1,0:T(8,128)S(1)} fusion(f32[7,32,128]{2,1,0:T(8,128)S(1)} %fusion.39, bf16[128,1024]{1,0:T(8,128)(2,1)} %param.2, s32[]{:T(128)S(6)} %select_n.3), kind=kOutput, calls=%fused_computation.44 | convolution fusion | flops 8388608 | bytes 344068 | tf_op jit(solution)/shard_map/dot_general | solution.py:26
  36.3 0.7 %fusion.22 = f32[7,8,128,128]{3,2,1,0:T(8,128)S(1)} fusion(f32[8,1024]{1,0:T(8,128)S(1)} %get-tuple-element.6, f32[128,1024]{1,0:T(8,128)S(1)} %convert_element_type.21, bf16[128,1024]{1,0:T(8,128)(2,1)S(1)} %collective-permute-done.5), kind=kOutput, calls=%fused_computation.24 | convolution fusion | flops 270532608 | bytes 1343488 | tf_op jit(solution)/shard_map/dot_general | solution.py:26
  37.0 0.7 %fusion.24 = f32[7,8,128,128]{3,2,1,0:T(8,128)S(1)} fusion(f32[7,8,128,128]{3,2,1,0:T(8,128)S(1)} %fusion.22, f32[8,1024]{1,0:T(8,128)S(1)} %get-tuple-element.6, f32[128,1024]{1,0:T(8,128)S(1)} %convert_element_type.21, bf16[128,1024]{1,0:T(8,128)(2,1)S(1)} %collective-permute-done.4), kind=kOutput, calls=%fused_computation.26 | convolution fusion | flops 270532608 | bytes 1343488 | tf_op jit(solution)/shard_map/dot_general | solution.py:26
  37.7 0.7 %fusion.26 = f32[7,8,128,128]{3,2,1,0:T(8,128)S(1)} fusion(f32[7,8,128,128]{3,2,1,0:T(8,128)S(1)} %fusion.24, f32[8,1024]{1,0:T(8,128)S(1)} %get-tuple-element.6, f32[128,1024]{1,0:T(8,128)S(1)} %convert_element_type.21, bf16[128,1024]{1,0:T(8,128)(2,1)S(1)} %collective-permute-done.3), kind=kOutput, calls=%fused_computation.28 | convolution fusion | flops 270532608 | bytes 1343488 | tf_op jit(solution)/shard_map/dot_general | solution.py:26
  38.8 0.7 %fusion.28 = f32[7,8,128,128]{3,2,1,0:T(8,128)S(1)} fusion(f32[7,8,128,128]{3,2,1,0:T(8,128)S(1)} %fusion.26, f32[8,1024]{1,0:T(8,128)S(1)} %get-tuple-element.6, f32[128,1024]{1,0:T(8,128)S(1)} %convert_element_type.21, bf16[128,1024]{1,0:T(8,128)(2,1)S(1)} %copy-done), kind=kOutput, calls=%fused_computation.30 | convolution fusion | flops 270532608 | bytes 1343488 | tf_op jit(solution)/shard_map/dot_general | solution.py:26
  39.8 9.8 %all_gather.3 = f32[7,128,128]{2,1,0:T(8,128)S(1)} all-gather(f32[7,32,128]{2,1,0:T(8,128)S(1)} %fusion.35), channel_id=1, replica_groups=mesh['vec'=8,'rep'=4] {'rep'}, dimensions={1}, use_global_device_ids=true | all-gather | bytes 573440 | tf_op jit(solution)/shard_map/all_gather | solution.py:62
  49.6 0.7 %fusion.30 = f32[7,8,128,128]{3,2,1,0:T(8,128)S(1)} fusion(f32[7,8,128,128]{3,2,1,0:T(8,128)S(1)} %fusion.28, f32[8,1024]{1,0:T(8,128)S(1)} %get-tuple-element.6, f32[128,1024]{1,0:T(8,128)S(1)} %convert_element_type.21, bf16[128,1024]{1,0:T(8,128)(2,1)S(1)} %collective-permute-done.6), kind=kOutput, calls=%fused_computation.32 | convolution fusion | flops 270532608 | bytes 1343488 | tf_op jit(solution)/shard_map/dot_general | solution.py:26
  50.3 0.7 %fusion.32 = f32[7,8,128,128]{3,2,1,0:T(8,128)S(1)} fusion(f32[7,8,128,128]{3,2,1,0:T(8,128)S(1)} %fusion.30, f32[8,1024]{1,0:T(8,128)S(1)} %get-tuple-element.6, f32[128,1024]{1,0:T(8,128)S(1)} %convert_element_type.21, bf16[128,1024]{1,0:T(8,128)(2,1)S(1)} %collective-permute-done.7), kind=kOutput, calls=%fused_computation.34 | convolution fusion | flops 270532608 | bytes 1343488 | tf_op jit(solution)/shard_map/dot_general | solution.py:26
  51.0 0.7 %fusion.34 = f32[7,8,128,128]{3,2,1,0:T(8,128)S(1)} fusion(f32[7,8,128,128]{3,2,1,0:T(8,128)S(1)} %fusion.32, f32[8,1024]{1,0:T(8,128)S(1)} %get-tuple-element.6, f32[128,1024]{1,0:T(8,128)S(1)} %convert_element_type.21, bf16[128,1024]{1,0:T(8,128)(2,1)S(1)} %collective-permute-done.8), kind=kOutput, calls=%fused_computation.36 | convolution fusion | flops 270532608 | bytes 1343488 | tf_op jit(solution)/shard_map/dot_general | solution.py:26
  51.7 1.9 %multiply_convert_fusion.8 = bf16[7,8,128,128]{3,2,1,0:T(8,128)(2,1)} fusion(f32[7,8,128,128]{3,2,1,0:T(8,128)S(1)} %fusion.34, f32[7,128,128]{2,1,0:T(8,128)S(1)} %all_gather.3, f32[8]{0:T(128)S(1)} %broadcast_multiply_fusion), kind=kLoop, calls=%fused_computation.8 | loop fusion | flops 3670016 | bytes 5963808 | tf_op jit(solution)/shard_map/convert_element_type | solution.py:66
  (19 shorter events, 2.7 us)
Async XLA Ops:
  0.0 9.0 %collective-permute-start.3 = (bf16[128,1024]{1,0:T(8,128)(2,1)}, bf16[128,1024]{1,0:T(8,128)(2,1)S(1)}, u32[]{:S(2)}, u32[]{:S(2)}) collective-permute-start(bf16[128,1024]{1,0:T(8,128)(2,1)} %param.2), channel_id=1, source_target_pairs={{28,0},{0,4},{4,8},{8,12},{12,16},{16,20},{20,24},{24,28},{29,1},{... | collective-permute-start | bytes 786440 | tf_op jit(solution)/shard_map/ppermute | solution.py:22
  0.5 21.0 %collective-permute-start.6 = (bf16[128,1024]{1,0:T(8,128)(2,1)}, bf16[128,1024]{1,0:T(8,128)(2,1)S(1)}, u32[]{:S(2)}, u32[]{:S(2)}) collective-permute-start(bf16[128,1024]{1,0:T(8,128)(2,1)} %param.2), channel_id=1, source_target_pairs={{4,0},{8,4},{12,8},{16,12},{20,16},{24,20},{28,24},{0,28},{5,1},{9... | collective-permute-start | bytes 786440 | tf_op jit(solution)/shard_map/ppermute | solution.py:22
  9.0 12.6 %collective-permute-start.4 = (bf16[128,1024]{1,0:T(8,128)(2,1)S(1)}, bf16[128,1024]{1,0:T(8,128)(2,1)S(1)}, u32[]{:S(2)}, u32[]{:S(2)}) collective-permute-start(bf16[128,1024]{1,0:T(8,128)(2,1)S(1)} %collective-permute-done.3), channel_id=1, source_target_pairs={{28,0},{0,4},{4,8},{8,12},{12,16},{16,20},{20,24},{24,28},{29,1},{... | collective-permute-start | bytes 786440 | tf_op jit(solution)/shard_map/ppermute | solution.py:22
  10.1 1.8 %collective-permute-start = (f32[8,1024]{1,0:T(8,128)S(1)}, f32[8,1024]{1,0:T(8,128)S(1)}, u32[]{:S(2)}, u32[]{:S(2)}) collective-permute-start(f32[8,1024]{1,0:T(8,128)S(1)} %fusion.56), channel_id=1, source_target_pairs={{0,4},{4,0},{8,12},{12,8},{16,20},{20,16},{24,28},{28,24},{1,5},{5... | collective-permute-start | bytes 98312 | tf_op jit(solution)/shard_map/ppermute | solution.py:14
  12.0 5.5 %collective-permute-start.1 = (f32[8,1024]{1,0:T(8,128)S(1)}, f32[8,1024]{1,0:T(8,128)S(1)}, u32[]{:S(2)}, u32[]{:S(2)}) collective-permute-start(f32[8,1024]{1,0:T(8,128)S(1)} %add.12), channel_id=1, source_target_pairs={{0,8},{4,12},{8,0},{12,4},{16,24},{20,28},{24,16},{28,20},{1,9},{5... | collective-permute-start | bytes 98312 | tf_op jit(solution)/shard_map/ppermute | solution.py:14
  17.5 4.9 %collective-permute-start.2 = (f32[8,1024]{1,0:T(8,128)S(1)}, f32[8,1024]{1,0:T(8,128)S(1)}, u32[]{:S(2)}, u32[]{:S(2)}) collective-permute-start(f32[8,1024]{1,0:T(8,128)S(1)} %add.13), channel_id=1, source_target_pairs={{0,16},{4,20},{8,24},{12,28},{16,0},{20,4},{24,8},{28,12},{1,17},{... | collective-permute-start | bytes 98312 | tf_op jit(solution)/shard_map/ppermute | solution.py:14
  21.5 6.8 %collective-permute-start.7 = (bf16[128,1024]{1,0:T(8,128)(2,1)S(1)}, bf16[128,1024]{1,0:T(8,128)(2,1)S(1)}, u32[]{:S(2)}, u32[]{:S(2)}) collective-permute-start(bf16[128,1024]{1,0:T(8,128)(2,1)S(1)} %collective-permute-done.6), channel_id=1, source_target_pairs={{4,0},{8,4},{12,8},{16,12},{20,16},{24,20},{28,24},{0,28},{5,1},{9... | collective-permute-start | bytes 786440 | tf_op jit(solution)/shard_map/ppermute | solution.py:22
  21.6 10.4 %collective-permute-start.5 = (bf16[128,1024]{1,0:T(8,128)(2,1)S(1)}, bf16[128,1024]{1,0:T(8,128)(2,1)S(1)}, u32[]{:S(2)}, u32[]{:S(2)}) collective-permute-start(bf16[128,1024]{1,0:T(8,128)(2,1)S(1)} %collective-permute-done.4), channel_id=1, source_target_pairs={{28,0},{0,4},{4,8},{8,12},{12,16},{16,20},{20,24},{24,28},{29,1},{... | collective-permute-start | bytes 786440 | tf_op jit(solution)/shard_map/ppermute | solution.py:22
  28.3 11.3 %collective-permute-start.8 = (bf16[128,1024]{1,0:T(8,128)(2,1)S(1)}, bf16[128,1024]{1,0:T(8,128)(2,1)S(1)}, u32[]{:S(2)}, u32[]{:S(2)}) collective-permute-start(bf16[128,1024]{1,0:T(8,128)(2,1)S(1)} %collective-permute-done.7), channel_id=1, source_target_pairs={{4,0},{8,4},{12,8},{16,12},{20,16},{24,20},{28,24},{0,28},{5,1},{9... | collective-permute-start | bytes 786440 | tf_op jit(solution)/shard_map/ppermute | solution.py:22
  36.3 2.2 %copy-start = (bf16[128,1024]{1,0:T(8,128)(2,1)S(1)}, bf16[128,1024]{1,0:T(8,128)(2,1)}, u32[]{:S(2)}) copy-start(bf16[128,1024]{1,0:T(8,128)(2,1)} %param.2) | copy-start | bytes 786436
